TPU v7x, 32 devices: a whole 2x2x4 slice. The times are simulated.
32 devices in a mesh: fsdp: 8 (over z, x), tensor: 2 (over y), dp: 2 (over core).
Axes of the slice: x: 2, y: 2, z: 4, core: 2. Of those that a mesh axis runs over, the one named last changes fastest.
Arguments:
- states: bfloat16 [4096, 4096], P('fsdp', ('tensor', 'dp')), may hold values from -6 to 6
- fresh_rows: bfloat16 [4096, 4096], P('fsdp', ('tensor', 'dp')), may hold values from -6 to 6
- norm_gain: bfloat16 [4096], P(('tensor', 'dp')), may hold values from 0.25 to 1.75
- gate_weight: bfloat16 [4096, 8192], P('fsdp', ('tensor', 'dp')), may hold values from -0.09375 to 0.09375
- up_weight: bfloat16 [4096, 8192], P('fsdp', ('tensor', 'dp')), may hold values from -0.09375 to 0.09375
- down_weight: bfloat16 [8192, 4096], P(('tensor', 'dp'), 'fsdp'), may hold values from -0.09375 to 0.09375
- halted: int32 [64, 64], P('fsdp'), may hold values from 0 to 1, as said below
- refill_index: int32 [64, 64], P('fsdp'), may hold values from 0 to 63, each once within a row
Outputs:
- next_states: bfloat16 [4096, 4096], P('fsdp', ('tensor', 'dp'))
Inputs may be any that keep to these rules, and one draw needn't show every extreme that they name: In each aligned block of 512 rows (in row order over all batches) at most 384 rows are running (halted 0), and some block has exactly 384 running rows. Each batch's row of refill_index holds every number of 0 to 63 once.
All inputs are finite; a program needn't handle non-finite values.
Results may differ from a plain program's by a relative error of at most 0.0085.
Values may be sent and summed in bfloat16 or wider, within the bound.
A program may use at most 128 MiB of HBM per device.

v0:
```python
import jax
import jax.numpy as jnp
from jax import lax
from jax.sharding import PartitionSpec as P

norm_eps = 1e-05


def block_update(source, norm_gain, gate_weight, up_weight, down_weight):
    gathered, gain_full = (
        lax.all_gather(source, ("tensor", "dp"), axis=1, tiled=True),
        lax.all_gather(norm_gain, ("tensor", "dp"), axis=0, tiled=True),
    )
    widened = gathered.astype(jnp.float32)
    mean_square = jnp.mean(widened * widened, axis=-1, keepdims=True)
    normed = (widened * lax.rsqrt(mean_square + norm_eps) * gain_full.astype(jnp.float32)).astype(
        jnp.bfloat16
    )
    gate_more = jnp.dot(
        normed,
        lax.all_gather(gate_weight, "fsdp", axis=0, tiled=True),
        preferred_element_type=jnp.float32,
    )
    up_more = jnp.dot(
        normed,
        lax.all_gather(up_weight, "fsdp", axis=0, tiled=True),
        preferred_element_type=jnp.float32,
    )
    hidden = (jax.nn.silu(gate_more) * up_more).astype(jnp.bfloat16)
    partial_value = jnp.dot(
        hidden,
        lax.all_gather(down_weight, "fsdp", axis=1, tiled=True),
        preferred_element_type=jnp.float32,
    )
    return lax.psum_scatter(
        partial_value.astype(jnp.bfloat16), ("tensor", "dp"), scatter_dimension=1, tiled=True
    ).astype(jnp.float32)


def body(states, fresh_rows, norm_gain, gate_weight, up_weight, down_weight, halted, refill_index):
    row_count = states.shape[0]
    running = halted.reshape(row_count) == 0
    capacity = row_count * 3 // 4
    slot_of = jnp.cumsum(running.astype(jnp.int32)) - 1
    slot_ids = lax.iota(jnp.int32, capacity)
    picker = ((slot_of[None, :] == slot_ids[:, None]) & running[None, :]).astype(jnp.bfloat16)
    source = jnp.dot(picker, states, preferred_element_type=jnp.float32).astype(jnp.bfloat16)
    compact = block_update(source, norm_gain, gate_weight, up_weight, down_weight)
    update = jnp.take(compact, jnp.clip(slot_of, 0, capacity - 1), axis=0)
    block_total = refill_index.shape[0]
    batch_len = refill_index.shape[1]
    fresh_blocks = fresh_rows.reshape(block_total, batch_len, fresh_rows.shape[1])
    refilled = jax.vmap(lambda block_rows, pick_index: block_rows[pick_index])(
        fresh_blocks, refill_index
    )
    refilled = refilled.reshape(row_count, fresh_rows.shape[1])
    computed = (states.astype(jnp.float32) + update).astype(jnp.bfloat16)
    return jnp.where(running[:, None], computed, refilled)


def solution(mesh):
    in_specs = (
        P("fsdp", ("tensor", "dp")),
        P("fsdp", ("tensor", "dp")),
        P(("tensor", "dp")),
        P("fsdp", ("tensor", "dp")),
        P("fsdp", ("tensor", "dp")),
        P(("tensor", "dp"), "fsdp"),
        P("fsdp", None),
        P("fsdp", None),
    )
    out_specs = P("fsdp", ("tensor", "dp"))
    return jax.shard_map(body, mesh=mesh, in_specs=in_specs, out_specs=out_specs, check_vma=False)
```

profile of v0, /device:TPU:0, one launch (start us, length us, event | category | flops | bytes accessed | tf_op | source)
XLA Modules:
  0.0 803.4 jit_solution(10444308348933228802)
XLA Ops:
  6.5 0.0 copy-start
  6.5 0.0 all-gather.5.cloned.1.call-start
  6.5 0.8 fusion.21
  7.3 0.1 reshape.107
  7.4 0.3 reduce-window.9
  7.7 0.1 slice.7
  7.8 0.1 slice_reduce_fusion
  7.9 0.1 compare_and_fusion
  8.0 0.1 eq.40
  8.1 2.7 convolution_convert_fusion.1
  10.8 0.0 all-gather.5.cloned.1.call-update
  10.8 0.0 copy-start.2
  10.8 0.0 all-gather.7.cloned.1.call-start
  10.9 0.7 all-gather.7.cloned.1.call-update
  11.6 0.0 all-gather.11.cloned.1.call-start
  11.6 0.7 all-gather.11.cloned.1.call-update
  12.3 0.0 all-gather.9.cloned.1.call-start
  12.4 0.5 all-gather.9.cloned.1.call-update
  12.9 0.0 reduce-scatter.2.cloned.1.call-start
  12.9 0.0 copy-done.2
  12.9 6.2 all_gather.16
  19.1 23.1 %all-gather.5.cloned.1.call-done = bf16[384,4096]{1,0:T(8,128)(2,1)} async-done(((bf16[384,1024]{1,0:T(8,128)(2,1)}), bf16[384,4096]{1,0:T(8,128)(2,1)}) %all-gather.5.cloned.1.call-update) | async-done | bytes 3145744 | tf_op jit(solution)/shard_map/all_gather | solution.py:11
  42.2 2.6 fusion
  44.8 226.8 %all-gather.7.cloned.1.call-done = bf16[4096,2048]{1,0:T(8,128)(2,1)} async-done(((bf16[512,2048]{1,0:T(8,128)(2,1)}), bf16[4096,2048]{1,0:T(8,128)(2,1)}) %all-gather.7.cloned.1.call-update) | async-done | bytes 16777232 | tf_op jit(solution)/shard_map/all_gather | solution.py:21
  271.6 12.3 %fusion.7 = f32[384,2048]{1,0:T(8,128)} fusion(bf16[4096,2048]{1,0:T(8,128)(2,1)} %all-gather.7.cloned.1.call-done, bf16[384,4096]{1,0:T(8,128)(2,1)} %all-gather.5.cloned.1.call-done, f32[4096]{0:T(1024)S(1)} %convert_element_type.40, f32[384]{0:T(512)S(1)} %add_rsqrt_fusion), kind=kOutput, calls=%fused_computation.13 | convolution fusion | flops 6448742400 | bytes 23086592 | tf_op jit(solution)/shard_map/dot_general | solution.py:19
  284.0 215.2 %all-gather.11.cloned.1.call-done = bf16[2048,4096]{1,0:T(8,128)(2,1)} async-done(((bf16[2048,512]{1,0:T(8,128)(2,1)}), bf16[2048,4096]{1,0:T(8,128)(2,1)}) %all-gather.11.cloned.1.call-update) | async-done | bytes 16777232 | tf_op jit(solution)/shard_map/all_gather | solution.py:32
  499.2 227.5 %all-gather.9.cloned.1.call-done = bf16[4096,2048]{1,0:T(8,128)(2,1)} async-done(((bf16[512,2048]{1,0:T(8,128)(2,1)}), bf16[4096,2048]{1,0:T(8,128)(2,1)}) %all-gather.9.cloned.1.call-update) | async-done | bytes 16777232 | tf_op jit(solution)/shard_map/all_gather | solution.py:26
  726.7 26.5 %convolution_convert_fusion = bf16[384,4096]{1,0:T(8,128)(2,1)} fusion(bf16[2048,4096]{1,0:T(8,128)(2,1)} %all-gather.11.cloned.1.call-done, f32[384,2048]{1,0:T(8,128)} %fusion.7, bf16[4096,2048]{1,0:T(8,128)(2,1)} %all-gather.9.cloned.1.call-done, bf16[384,4096]{1,0:T(8,128)(2,1)} %all-gather.5.cloned.1.call-done, f32[4096]{0:T(1024)S(1)} %convert_element_type.40, ...), kind=kOutput, calls=%fused_computation.7 | convolution fusion | flops 12897484800 | bytes 43009536 | tf_op jit(solution)/shard_map/dot_general | solution.py:30
  753.2 0.0 copy-start.1
  753.2 0.0 reduce-scatter.2.cloned.1.call-update
  753.2 0.7 copy-done.1
  753.9 0.1 reshape.116
  753.9 0.0 copy-done
  754.0 7.9 gather_fusion.1
  761.9 0.1 fusion.17
  762.0 27.3 %reduce-scatter.2.cloned.1.call-done = bf16[384,1024]{1,0:T(8,128)(2,1)} async-done(((bf16[384,4096]{1,0:T(8,128)(2,1)}), bf16[384,1024]{1,0:T(8,128)(2,1)}) %reduce-scatter.2.cloned.1.call-update) | async-done | bytes 786448 | tf_op jit(solution)/shard_map/reduce_scatter | solution.py:35
  789.3 1.3 convert_element_type.44
  790.6 2.7 gather_fusion
  793.3 3.6 fusion.4
  (6 shorter events, 0.1 us)
Async XLA Ops:
  6.5 747.4 %copy-start = (bf16[512,1024]{1,0:T(8,128)(2,1)S(1)}, bf16[512,1024]{1,0:T(8,128)(2,1)}, u32[]{:S(2)}) copy-start(bf16[512,1024]{1,0:T(8,128)(2,1)} %param.9) | copy-start | bytes 3145732
  6.5 35.7 %all-gather.5.cloned.1.call-start = ((), (), s32[]{:S(2)}) async-start(), calls=%async_computation.1 | async-start | bytes 3932160 | tf_op jit(solution)/shard_map/all_gather | solution.py:11
  10.8 2.1 copy-start.2
  10.8 260.8 %all-gather.7.cloned.1.call-start = ((), (), s32[]{:S(2)}) async-start(), calls=%async_computation.2 | async-start | bytes 18874368 | tf_op jit(solution)/shard_map/all_gather | solution.py:21
  11.6 487.6 %all-gather.11.cloned.1.call-start = ((), (), s32[]{:S(2)}) async-start(), calls=%async_computation.4 | async-start | bytes 18874368 | tf_op jit(solution)/shard_map/all_gather | solution.py:32
  12.3 714.4 %all-gather.9.cloned.1.call-start = ((), (), s32[]{:S(2)}) async-start(), calls=%async_computation.3 | async-start | bytes 18874368 | tf_op jit(solution)/shard_map/all_gather | solution.py:26
  12.9 776.4 %reduce-scatter.2.cloned.1.call-start = ((), (), s32[]{:S(2)}) async-start(), calls=%async_computation.5 | async-start | bytes 3932160 | tf_op jit(solution)/shard_map/reduce_scatter | solution.py:35
  753.2 0.7 copy-start.1
Sparse Core Ops, SparseCore 0:
  10.9 31.2 all-gather.4
  44.3 227.2 all-gather.6
  273.7 225.4 all-gather.10
  501.2 225.4 all-gather.8
  753.3 35.9 reduce-scatter.1
where the time goes:
time: 804 us; the launch traced here: 803 us
  waiting for transfers between devices  722 us (90%)
  matrix products  41.5 us (5%)
  between operations  13.2 us (2%)
  local copies, waits for them, and re-layouts  11.7 us (1%)
  other arithmetic  8.79 us (1%)
    all_gather x1, waiting for transfers between devices, block_update(): lax.all_gather(up_weight, 'fsdp', axis=0, tiled=True)  227 us
    all_gather x1, waiting for transfers between devices, block_update(): lax.all_gather(gate_weight, 'fsdp', axis=0, tiled=True)  227 us
    all_gather x1, waiting for transfers between devices, block_update(): lax.all_gather(down_weight, 'fsdp', axis=1, tiled=True)  215 us
    reduce_scatter x1, waiting for transfers between devices, block_update(): lax.psum_scatter(partial_value.astype(jnp.bfloat16), ('tensor', 'dp'), sc...  27.3 us
    dot_general x1, matrix products, block_update(): jnp.dot(hidden, lax.all_gather(down_weight, 'fsdp', axis=1, tiled=True),...  26.5 us
    all_gather x1, waiting for transfers between devices, block_update(): lax.all_gather(source, ('tensor', 'dp'), axis=1, tiled=True)  23.1 us
  transfers between devices with their start and end apart: 5, of which 5 were waited for; matrix products, arithmetic and copies ran while one was open for 3% of the time, Pallas kernels for 0%

commit v1 on v0

--- a/solution.py
+++ b/solution.py
@@ -4,6 +4,19 @@
 from jax.sharding import PartitionSpec as P
 
 norm_eps = 1e-05
+
+
+def collect(x, axis, dim):
+    length, place, rows = (lax.axis_size(axis), lax.axis_index(axis), x.shape[dim])
+    right = [(i, (i + 1) % length) for i in range(length)]
+    filled = jnp.zeros((*x.shape[:dim], length * rows, *x.shape[dim + 1 :]), x.dtype)
+    block = x
+    for hop in range(length):
+        owner = (place - hop) % length
+        filled = lax.dynamic_update_slice_in_dim(filled, block, owner * rows, axis=dim)
+        if hop < length - 1:
+            block = lax.ppermute(block, axis, right)
+    return filled
 
 
 def block_update(source, norm_gain, gate_weight, up_weight, down_weight):
@@ -16,11 +29,7 @@
     normed = (widened * lax.rsqrt(mean_square + norm_eps) * gain_full.astype(jnp.float32)).astype(
         jnp.bfloat16
     )
-    gate_more = jnp.dot(
-        normed,
-        lax.all_gather(gate_weight, "fsdp", axis=0, tiled=True),
-        preferred_element_type=jnp.float32,
-    )
+    gate_more = jnp.dot(normed, collect(gate_weight, "fsdp", 0), preferred_element_type=jnp.float32)
     up_more = jnp.dot(
         normed,
         lax.all_gather(up_weight, "fsdp", axis=0, tiled=True),

time: 804 us -> 822 us (1.022)
  local copies, waits for them, and re-layouts: 11.7 us -> 40.6 us
  waiting for transfers between devices: 722 us -> 708 us
    ppermute x0 -> x7, waiting for transfers between devices: none -> 568 us  [collect(): block = lax.ppermute(block, axis, right)]
    all_gather x1, waiting for transfers between devices: 227 us -> 0.01 us  [block_update(): lax.all_gather(up_weight, 'fsdp', axis=0, tiled=True)]
    all_gather x1 -> x0, waiting for transfers between devices: 227 us -> none  [block_update(): lax.all_gather(gate_weight, 'fsdp', axis=0, tiled=True)]
    all_gather x1, waiting for transfers between devices: 215 us -> 110 us  [block_update(): lax.all_gather(down_weight, 'fsdp', axis=1, tiled=True)]
    all_gather x1, waiting for transfers between devices: 23.1 us -> 0.01 us  [block_update(): lax.all_gather(source, ('tensor', 'dp'), axis=1, tiled=True)]
    dynamic_update_slice x0 -> x8, local copies, waits for them, and re-layouts: none -> 17.2 us  [collect(): lax.dynamic_update_slice_in_dim(filled, block, owner * rows, axis=dim)]
  transfers between devices with their start and end apart: 5 -> 11, of which waited for: 5 -> 9; matrix products, arithmetic and copies ran while one was open for 3% -> 6% of each run, Pallas kernels for 0% -> 0%
where the time goes in v1:
time: 822 us
  waiting for transfers between devices  708 us (86%)
  matrix products  41.6 us (5%)
  local copies, waits for them, and re-layouts  40.6 us (5%)
  between operations  13.2 us (2%)
  other arithmetic  8.94 us (1%)
    ppermute x7, waiting for transfers between devices, collect(): block = lax.ppermute(block, axis, right)  568 us
    all_gather x1, waiting for transfers between devices, block_update(): lax.all_gather(down_weight, 'fsdp', axis=1, tiled=True)  110 us
    reduce_scatter x1, waiting for transfers between devices, block_update(): lax.psum_scatter(partial_value.astype(jnp.bfloat16), ('tensor', 'dp'), sc...  28 us
    dot_general x1, matrix products, block_update(): jnp.dot(hidden, lax.all_gather(down_weight, 'fsdp', axis=1, tiled=True),...  26.3 us
    dynamic_update_slice x8, local copies, waits for them, and re-layouts, collect(): lax.dynamic_update_slice_in_dim(filled, block, owner * rows, axis=dim)  17.2 us
  transfers between devices with their start and end apart: 11, of which 9 were waited for; matrix products, arithmetic and copies ran while one was open for 6% of the time, Pallas kernels for 0%

profile of v1, /device:TPU:0, one launch (start us, length us, event | category | flops | bytes accessed | tf_op | source)
XLA Modules:
  0.0 821.6 jit_solution(4628258196972856042)
XLA Ops:
  6.5 0.0 copy-start
  6.5 0.0 all-gather.4.cloned.1.call-start
  6.5 0.8 fusion.25
  7.3 0.1 reshape.107
  7.4 0.3 reduce-window.9
  7.7 0.1 slice.7
  7.8 0.1 slice_reduce_fusion
  7.9 0.1 compare_and_fusion
  8.0 0.1 eq.49
  8.1 2.8 convolution_convert_fusion.1
  10.9 0.0 all-gather.4.cloned.1.call-update
  11.0 0.0 all-gather.6.cloned.1.call-start
  11.0 0.7 all-gather.6.cloned.1.call-update
  11.7 0.0 all-gather.8.cloned.1.call-start
  11.8 0.7 all-gather.8.cloned.1.call-update
  12.5 0.0 reduce-scatter.2.cloned.1.call-start
  12.5 0.0 copy-done.1
  12.5 3.0 collective-permute-start
  15.5 53.7 %collective-permute-done = bf16[512,2048]{1,0:T(8,128)(2,1)S(1)} collective-permute-done((bf16[512,2048]{1,0:T(8,128)(2,1)S(1)}, bf16[512,2048]{1,0:T(8,128)(2,1)S(1)}, u32[]{:S(2)}, u32[]{:S(2)}) %collective-permute-start) | collective-permute-done | bytes 2097184 | tf_op jit(solution)/shard_map/ppermute | solution.py:18
  69.2 0.6 collective-permute-start.1
  69.9 0.7 copy-done.4
  70.5 93.7 %collective-permute-done.1 = bf16[512,2048]{1,0:T(8,128)(2,1)S(1)} collective-permute-done((bf16[512,2048]{1,0:T(8,128)(2,1)S(1)}, bf16[512,2048]{1,0:T(8,128)(2,1)S(1)}, u32[]{:S(2)}, u32[]{:S(2)}) %collective-permute-start.1) | collective-permute-done | bytes 2097184 | tf_op jit(solution)/shard_map/ppermute | solution.py:18
  164.3 0.0 collective-permute-start.2
  164.3 1.3 copy-done.8
  165.6 83.8 %collective-permute-done.2 = bf16[512,2048]{1,0:T(8,128)(2,1)S(1)} collective-permute-done((bf16[512,2048]{1,0:T(8,128)(2,1)S(1)}, bf16[512,2048]{1,0:T(8,128)(2,1)S(1)}, u32[]{:S(2)}, u32[]{:S(2)}) %collective-permute-start.2) | collective-permute-done | bytes 2097184 | tf_op jit(solution)/shard_map/ppermute | solution.py:18
  249.3 1.4 copy-done.2
  250.7 0.0 collective-permute-start.3
  250.7 95.0 %collective-permute-done.3 = bf16[512,2048]{1,0:T(8,128)(2,1)S(1)} collective-permute-done((bf16[512,2048]{1,0:T(8,128)(2,1)S(1)}, bf16[512,2048]{1,0:T(8,128)(2,1)S(1)}, u32[]{:S(2)}, u32[]{:S(2)}) %collective-permute-start.3) | collective-permute-done | bytes 2097184 | tf_op jit(solution)/shard_map/ppermute | solution.py:18
  345.7 1.3 copy-done.6
  347.0 0.0 collective-permute-start.4
  347.0 99.5 %collective-permute-done.4 = bf16[512,2048]{1,0:T(8,128)(2,1)} collective-permute-done((bf16[512,2048]{1,0:T(8,128)(2,1)S(1)}, bf16[512,2048]{1,0:T(8,128)(2,1)}, u32[]{:S(2)}, u32[]{:S(2)}) %collective-permute-start.4) | collective-permute-done | bytes 2097184 | tf_op jit(solution)/shard_map/ppermute | solution.py:18
  446.5 0.0 collective-permute-start.5
  446.5 0.0 copy-done.11
  446.5 5.2 all_gather.13
  451.7 7.0 broadcast_in_dim.32
  458.8 1.6 constant_dynamic-update-slice_fusion.7
  460.3 71.7 %collective-permute-done.5 = bf16[512,2048]{1,0:T(8,128)(2,1)} collective-permute-done((bf16[512,2048]{1,0:T(8,128)(2,1)}, bf16[512,2048]{1,0:T(8,128)(2,1)}, u32[]{:S(2)}, u32[]{:S(2)}) %collective-permute-start.5) | collective-permute-done | bytes 2097184 | tf_op jit(solution)/shard_map/ppermute | solution.py:18
  532.0 0.0 collective-permute-start.6
  532.0 0.0 copy-done.5
  532.0 1.5 constant_dynamic-update-slice_fusion.6
  533.5 0.0 copy-done.9
  533.5 1.5 constant_dynamic-update-slice_fusion.5
  535.0 2.7 fusion
  537.7 0.0 copy-done.3
  537.7 1.6 constant_dynamic-update-slice_fusion.4
  539.3 0.0 copy-done.7
  539.3 1.5 constant_dynamic-update-slice_fusion.3
  540.8 3.2 constant_dynamic-update-slice_fusion.2
  544.0 3.1 constant_dynamic-update-slice_fusion.1
  547.2 71.0 %collective-permute-done.6 = bf16[512,2048]{1,0:T(8,128)(2,1)} collective-permute-done((bf16[512,2048]{1,0:T(8,128)(2,1)}, bf16[512,2048]{1,0:T(8,128)(2,1)}, u32[]{:S(2)}, u32[]{:S(2)}) %collective-permute-start.6) | collective-permute-done | bytes 2097184 | tf_op jit(solution)/shard_map/ppermute | solution.py:18
  618.2 3.2 constant_dynamic-update-slice_fusion
  621.5 12.5 %fusion.5 = f32[384,2048]{1,0:T(8,128)} fusion(bf16[4096,2048]{1,0:T(8,128)(2,1)} %all-gather.6.cloned.1.call-done, bf16[384,4096]{1,0:T(8,128)(2,1)} %all-gather.4.cloned.1.call-done, f32[4096]{0:T(1024)S(1)} %convert_element_type.40, f32[384]{0:T(512)S(1)} %add_rsqrt_fusion), kind=kOutput, calls=%fused_computation.13 | convolution fusion | flops 6448742400 | bytes 23086592 | tf_op jit(solution)/shard_map/dot_general | solution.py:33
  633.9 110.5 %all-gather.8.cloned.1.call-done = bf16[2048,4096]{1,0:T(8,128)(2,1)} async-done(((bf16[2048,512]{1,0:T(8,128)(2,1)}), bf16[2048,4096]{1,0:T(8,128)(2,1)}) %all-gather.8.cloned.1.call-update) | async-done | bytes 16777232 | tf_op jit(solution)/shard_map/all_gather | solution.py:41
  744.4 26.3 %convolution_convert_fusion = bf16[384,4096]{1,0:T(8,128)(2,1)} fusion(bf16[2048,4096]{1,0:T(8,128)(2,1)} %all-gather.8.cloned.1.call-done, f32[384,2048]{1,0:T(8,128)} %fusion.5, bf16[4096,2048]{1,0:T(8,128)(2,1)} %constant_dynamic-update-slice_fusion, bf16[384,4096]{1,0:T(8,128)(2,1)} %all-gather.4.cloned.1.call-done, f32[4096]{0:T(1024)S(1)} %convert_element_type.40, ...), kind=kOutput, calls=%fused_computation.7 | convolution fusion | flops 12897484800 | bytes 43009536 | tf_op jit(solution)/shard_map/dot_general | solution.py:39
  770.7 0.0 reduce-scatter.2.cloned.1.call-update
  770.7 0.7 copy-done.10
  771.4 0.1 reshape.116
  771.5 0.0 copy-done
  771.5 7.9 gather_fusion.1
  779.4 0.1 fusion.21
  779.5 28.0 %reduce-scatter.2.cloned.1.call-done = bf16[384,1024]{1,0:T(8,128)(2,1)} async-done(((bf16[384,4096]{1,0:T(8,128)(2,1)}), bf16[384,1024]{1,0:T(8,128)(2,1)}) %reduce-scatter.2.cloned.1.call-update) | async-done | bytes 786448 | tf_op jit(solution)/shard_map/reduce_scatter | solution.py:44
  807.5 1.3 convert_element_type.44
  808.8 2.7 gather_fusion
  811.5 3.6 fusion.4
  (19 shorter events, 0.1 us)
Async XLA Ops:
  6.5 764.9 %copy-start = (bf16[512,1024]{1,0:T(8,128)(2,1)S(1)}, bf16[512,1024]{1,0:T(8,128)(2,1)}, u32[]{:S(2)}) copy-start(bf16[512,1024]{1,0:T(8,128)(2,1)} %param.9) | copy-start | bytes 3145732
  6.5 528.5 %all-gather.4.cloned.1.call-start = ((), (), s32[]{:S(2)}) async-start(), calls=%async_computation.1 | async-start | bytes 3932160 | tf_op jit(solution)/shard_map/all_gather | solution.py:24
  8.1 4.4 copy-start.1
  10.9 435.6 %copy-start.11 = (bf16[1024]{0:T(1024)(128)(2,1)S(1)}, bf16[1024]{0:T(1024)(128)(2,1)}, u32[]{:S(2)}) copy-start(bf16[1024]{0:T(1024)(128)(2,1)} %param.10) | copy-start | bytes 6148
  11.0 610.5 %all-gather.6.cloned.1.call-start = ((), (), s32[]{:S(2)}) async-start(), calls=%async_computation.2 | async-start | bytes 18874368 | tf_op jit(solution)/shard_map/all_gather | solution.py:35
  11.7 732.7 %all-gather.8.cloned.1.call-start = ((), (), s32[]{:S(2)}) async-start(), calls=%async_computation.3 | async-start | bytes 18874368 | tf_op jit(solution)/shard_map/all_gather | solution.py:41
  12.5 795.0 %reduce-scatter.2.cloned.1.call-start = ((), (), s32[]{:S(2)}) async-start(), calls=%async_computation.4 | async-start | bytes 3932160 | tf_op jit(solution)/shard_map/reduce_scatter | solution.py:44
  12.5 56.7 %collective-permute-start = (bf16[512,2048]{1,0:T(8,128)(2,1)S(1)}, bf16[512,2048]{1,0:T(8,128)(2,1)S(1)}, u32[]{:S(2)}, u32[]{:S(2)}) collective-permute-start(bf16[512,2048]{1,0:T(8,128)(2,1)S(1)} %copy-done.1), channel_id=1, source_target_pairs={{0,4},{4,8},{8,12},{12,16},{16,20},{20,24},{24,28},{28,0},{1,5},{5... | collective-permute-start | bytes 6291464 | tf_op jit(solution)/shard_map/ppermute | solution.py:18
  69.2 1.3 copy-start.4
  69.2 95.0 %collective-permute-start.1 = (bf16[512,2048]{1,0:T(8,128)(2,1)S(1)}, bf16[512,2048]{1,0:T(8,128)(2,1)S(1)}, u32[]{:S(2)}, u32[]{:S(2)}) collective-permute-start(bf16[512,2048]{1,0:T(8,128)(2,1)S(1)} %collective-permute-done), channel_id=1, source_target_pairs={{0,4},{4,8},{8,12},{12,16},{16,20},{20,24},{24,28},{28,0},{1,5},{5... | collective-permute-start | bytes 6291464 | tf_op jit(solution)/shard_map/ppermute | solution.py:18
  164.3 1.3 copy-start.8
  164.3 85.1 %collective-permute-start.2 = (bf16[512,2048]{1,0:T(8,128)(2,1)S(1)}, bf16[512,2048]{1,0:T(8,128)(2,1)S(1)}, u32[]{:S(2)}, u32[]{:S(2)}) collective-permute-start(bf16[512,2048]{1,0:T(8,128)(2,1)S(1)} %collective-permute-done.1), channel_id=1, source_target_pairs={{0,4},{4,8},{8,12},{12,16},{16,20},{20,24},{24,28},{28,0},{1,5},{5... | collective-permute-start | bytes 6291464 | tf_op jit(solution)/shard_map/ppermute | solution.py:18
  249.3 1.4 copy-start.2
  250.7 95.0 %collective-permute-start.3 = (bf16[512,2048]{1,0:T(8,128)(2,1)S(1)}, bf16[512,2048]{1,0:T(8,128)(2,1)S(1)}, u32[]{:S(2)}, u32[]{:S(2)}) collective-permute-start(bf16[512,2048]{1,0:T(8,128)(2,1)S(1)} %collective-permute-done.2), channel_id=1, source_target_pairs={{0,4},{4,8},{8,12},{12,16},{16,20},{20,24},{24,28},{28,0},{1,5},{5... | collective-permute-start | bytes 6291464 | tf_op jit(solution)/shard_map/ppermute | solution.py:18
  345.7 1.3 copy-start.6
  347.0 99.5 %collective-permute-start.4 = (bf16[512,2048]{1,0:T(8,128)(2,1)S(1)}, bf16[512,2048]{1,0:T(8,128)(2,1)}, u32[]{:S(2)}, u32[]{:S(2)}) collective-permute-start(bf16[512,2048]{1,0:T(8,128)(2,1)S(1)} %collective-permute-done.3), channel_id=1, source_target_pairs={{0,4},{4,8},{8,12},{12,16},{16,20},{20,24},{24,28},{28,0},{1,5},{5... | collective-permute-start | bytes 6291464 | tf_op jit(solution)/shard_map/ppermute | solution.py:18
  446.5 85.5 %collective-permute-start.5 = (bf16[512,2048]{1,0:T(8,128)(2,1)}, bf16[512,2048]{1,0:T(8,128)(2,1)}, u32[]{:S(2)}, u32[]{:S(2)}) collective-permute-start(bf16[512,2048]{1,0:T(8,128)(2,1)} %collective-permute-done.4), channel_id=1, source_target_pairs={{0,4},{4,8},{8,12},{12,16},{16,20},{20,24},{24,28},{28,0},{1,5},{5... | collective-permute-start | bytes 6291464 | tf_op jit(solution)/shard_map/ppermute | solution.py:18
  458.8 73.3 %copy-start.5 = (bf16[512,2048]{1,0:T(8,128)(2,1)S(1)}, bf16[512,2048]{1,0:T(8,128)(2,1)}, u32[]{:S(2)}) copy-start(bf16[512,2048]{1,0:T(8,128)(2,1)} %copy-done.4) | copy-start | bytes 6291460
  460.3 73.2 %copy-start.9 = (bf16[512,2048]{1,0:T(8,128)(2,1)S(1)}, bf16[512,2048]{1,0:T(8,128)(2,1)}, u32[]{:S(2)}) copy-start(bf16[512,2048]{1,0:T(8,128)(2,1)} %copy-done.8) | copy-start | bytes 6291460
  532.0 86.2 %collective-permute-start.6 = (bf16[512,2048]{1,0:T(8,128)(2,1)}, bf16[512,2048]{1,0:T(8,128)(2,1)}, u32[]{:S(2)}, u32[]{:S(2)}) collective-permute-start(bf16[512,2048]{1,0:T(8,128)(2,1)} %collective-permute-done.5), channel_id=1, source_target_pairs={{0,4},{4,8},{8,12},{12,16},{16,20},{20,24},{24,28},{28,0},{1,5},{5... | collective-permute-start | bytes 6291464 | tf_op jit(solution)/shard_map/ppermute | solution.py:18
  533.5 4.2 copy-start.3
  535.0 4.3 copy-start.7
  770.7 0.7 copy-start.10
Sparse Core Ops, SparseCore 0:
  11.1 31.2 all-gather.3
  44.5 358.0 all-gather.5
  404.6 339.7 all-gather.7
  770.8 36.6 reduce-scatter.1
